TPU v7x, 32 devices: a whole 2x2x4 slice. The times are simulated.
32 devices in a mesh: section: 4 (over z), dp: 8 (over y, x, core).
Axes of the slice: x: 2, y: 2, z: 4, core: 2. Of those that a mesh axis runs over, the one named last changes fastest.
Arguments:
- tokens: bfloat16 [64, 32, 3584], P('dp'), may hold values from -6 to 6
- lengths: int32 [64], P('dp'), may hold values from 1 to 32
- assign: int32 [64, 2], P('dp'), may hold values from 0 to 7, as said below
- group_ids: int32 [64], P('dp'), may hold values from 0 to 7
- rewards: float32 [64], P('dp'), may hold values from -6 to 6
- norm_gain: bfloat16 [4, 3584], P('section'), may hold values from 0.5 to 1.5
- w_query: bfloat16 [4, 3584, 1792], P('section', 'dp'), may hold values from -0.09375 to 0.09375
- w_keyval: bfloat16 [4, 3584, 512], P('section', 'dp'), may hold values from -0.09375 to 0.09375
- w_out: bfloat16 [4, 1792, 3584], P('section', 'dp'), may hold values from -0.125 to 0.125
Outputs:
- hidden: bfloat16 [16, 128, 3584], P('dp', None, 'section')
- token_adv: bfloat16 [16, 128], P('dp')
Inputs may be any that keep to these rules, and one draw needn't show every extreme that they name: assign[g,0] is one of the 4 dp indices from the sequence's own upward, wrapping; each dp index sends exactly 2 sequences to each of them; assign[g,1] is a row of the owner, and every row of every owner receives exactly 4 sequences.
All inputs are finite; a program needn't handle non-finite values.
Results may differ from a plain program's by a relative error of at most 0.014.
Values may be sent and summed in bfloat16 or wider, within the bound.
A program may use at most 128 MiB of HBM per device.

v0:
```python
import math
import jax
import jax.numpy as jnp
from jax import lax
from jax.sharding import PartitionSpec as P

HEAD = 128
ROW = 128
SPREAD = 4
GROUP_AVG = 8
ROWS_DEV = 2
CAP = 2
EPS = 1e-06
THETA = 1000000.0


def entering(shard, axis, combine, identity):
    length, place = (lax.axis_size(axis), lax.axis_index(axis))
    everything = lax.all_gather(shard, axis)
    start = jnp.broadcast_to(jnp.asarray(identity, shard.dtype), shard.shape)

    def hop(k, before):
        reached = k < place
        new = combine(before, everything[k])
        return jnp.where(reached, new, before)

    return lax.fori_loop(0, length, hop, start)


def from_behind(block, axis, distance):
    devices = range(lax.axis_size(axis))
    route = [((i - distance) % len(devices), i) for i in devices]
    return lax.ppermute(block, axis, route)


def shifted(shard, axis, by):
    length = lax.axis_size(axis)
    pairs = [(i, i + by) for i in range(length) if 0 <= i + by < length]
    return lax.ppermute(shard, axis, pairs)


def spread(value, axis, source):
    kept = jnp.where(lax.axis_index(axis) == source, value, 0).astype(value.dtype)
    return lax.psum(kept, axis)


def rotate(inputs, position):
    half_size = inputs.shape[-1] // 2
    inverse = THETA ** (-(jnp.arange(half_size, dtype=jnp.float32) * 2.0 / inputs.shape[-1]))
    angles = position.astype(jnp.float32)[..., None] * inverse
    cosine = jnp.cos(angles)[:, :, None, :]
    sine_part = jnp.sin(angles)[:, :, None, :]
    first_half = inputs[..., :half_size]
    second = inputs[..., half_size:]
    return jnp.concatenate(
        [first_half * cosine - second * sine_part, second * cosine + first_half * sine_part], -1
    )


def attend_block(rows_in, segment, position, gain_row, query_full, keyval_full, out_full):
    count, row_len, width = rows_in.shape
    wide_in = rows_in.astype(jnp.float32)
    variance = jnp.mean(wide_in * wide_in, -1, keepdims=True)
    normed = (wide_in * lax.rsqrt(variance + EPS) * gain_row.astype(jnp.float32)).astype(
        jnp.bfloat16
    )
    normed = normed.reshape(count * row_len, width)
    head_count = query_full.shape[1] // HEAD
    kv_count = keyval_full.shape[1] // (2 * HEAD)
    per_group = head_count // kv_count
    queries = jnp.dot(normed, query_full, preferred_element_type=jnp.float32).reshape(
        count, row_len, head_count, HEAD
    )
    queries = rotate(queries, position).astype(jnp.bfloat16)
    keyval = jnp.dot(normed, keyval_full, preferred_element_type=jnp.float32).reshape(
        count, row_len, 2, kv_count, HEAD
    )
    key_rows = rotate(keyval[:, :, 0], position).astype(jnp.bfloat16)
    value_rows = keyval[:, :, 1].astype(jnp.bfloat16)
    grouped = queries.reshape(count, row_len, kv_count, per_group, HEAD)
    scores = jnp.einsum(
        "nqkgd,nskd->nkgqs", grouped, key_rows, preferred_element_type=jnp.float32
    ) / math.sqrt(HEAD)
    columns = jnp.arange(row_len)
    allowed = (segment[:, :, None] == segment[:, None, :]) & (
        columns[None, None, :] <= columns[None, :, None]
    )
    scores = jnp.where(allowed[:, None, None], scores, -1e30)
    top_score = jnp.max(scores, -1, keepdims=True)
    expo = jnp.exp(scores - top_score)
    weights = (expo / jnp.sum(expo, -1, keepdims=True)).astype(jnp.bfloat16)
    mixed_heads = jnp.einsum(
        "nkgqs,nskd->nqkgd", weights, value_rows, preferred_element_type=jnp.float32
    )
    mixed_heads = mixed_heads.astype(jnp.bfloat16).reshape(count * row_len, head_count * HEAD)
    updated = wide_in + jnp.dot(mixed_heads, out_full, preferred_element_type=jnp.float32).reshape(
        count, row_len, width
    )
    return updated.astype(jnp.bfloat16)


def body(tokens, lengths, assign, group_ids, rewards, norm_gain, w_query, w_keyval, w_out):
    seq_dev, lmax_len, width = tokens.shape
    dp_count = lax.axis_size("dp")
    sections = lax.axis_size("section")
    dp_index = lax.axis_index("dp")
    section_me = lax.axis_index("section")
    rows_dev = ROWS_DEV
    groups_all = seq_dev * dp_count // GROUP_AVG
    member = (group_ids[:, None] == jnp.arange(groups_all, dtype=jnp.int32)[None, :]).astype(
        jnp.float32
    )
    group_sums = jnp.sum(member * rewards[:, None], 0)
    counts = jnp.sum(member, 0)
    group_sums, counts = lax.psum((group_sums, counts), "dp")
    group_mean = group_sums / jnp.maximum(counts, 1.0)
    adv = (rewards - jnp.sum(member * group_mean[None, :], 1)).astype(jnp.bfloat16)
    owners = assign[:, 0]
    target_row = assign[:, 1]
    reach = (owners - dp_index) % dp_count
    local_ids = jnp.arange(seq_dev, dtype=jnp.int32)
    earlier = local_ids[None, :] < local_ids[:, None]
    packed_row = owners * rows_dev + target_row
    total_rows = dp_count * rows_dev
    hit = (packed_row[:, None] == jnp.arange(total_rows, dtype=jnp.int32)[None, :]).astype(
        jnp.int32
    )
    fill = jnp.sum(hit * lengths[:, None], 0)
    before = entering(fill, "dp", lambda lower, upper: lower + upper, jnp.zeros_like(fill))
    same_row = ((packed_row[:, None] == packed_row[None, :]) & earlier).astype(jnp.int32)
    labels = jnp.sum(hit * before[None, :], 1) + jnp.sum(same_row * lengths[None, :], 1)
    rank_in = jnp.sum(((reach[:, None] == reach[None, :]) & earlier).astype(jnp.int32), 1)
    slot_ids = reach * CAP + rank_in
    picked = (slot_ids[None, :] == local_ids[:, None]).astype(jnp.int32)
    source_of = jnp.sum(picked * local_ids[None, :], 1)
    send_tok = tokens[source_of]
    send_adv = adv[source_of]
    send_lab = jnp.stack([target_row, lengths, labels], 1).astype(jnp.int32)[source_of]
    got_tok = []
    got_adv = []
    got_lab = []
    for reach_step in range(SPREAD):
        low_end = reach_step * CAP
        tok_piece = send_tok[low_end : low_end + CAP]
        adv_piece = send_adv[low_end : low_end + CAP]
        lab_piece = send_lab[low_end : low_end + CAP]
        if reach_step > 0:
            tok_piece, adv_piece = from_behind((tok_piece, adv_piece), "dp", reach_step)
            lab_piece = from_behind(lab_piece, "dp", reach_step)
        got_tok.append(tok_piece)
        got_adv.append(adv_piece)
        got_lab.append(lab_piece)
    recv_tok = jnp.concatenate(got_tok, 0)
    recv_adv = jnp.concatenate(got_adv, 0)
    recv_lab = jnp.concatenate(got_lab, 0)
    recv_row = recv_lab[:, 0]
    recv_len = recv_lab[:, 1]
    recv_off = recv_lab[:, 2]
    cell_ids = jnp.arange(rows_dev * ROW, dtype=jnp.int32)
    cell_row = cell_ids // ROW
    cell_col = cell_ids % ROW
    inside_at = cell_col[None, :] - recv_off[:, None]
    matched = (
        (recv_row[:, None] == cell_row[None, :])
        & (inside_at >= 0)
        & (inside_at < recv_len[:, None])
    )
    matched_int = matched.astype(jnp.int32)
    filled = jnp.sum(matched_int, 0) > 0
    anchor = jnp.sum(matched_int * (local_ids[:, None] * lmax_len + inside_at), 0)
    flat_tok = recv_tok.reshape(seq_dev * lmax_len, width)
    packed = jnp.where(filled[:, None], flat_tok[anchor], jnp.zeros((), jnp.bfloat16)).reshape(
        rows_dev, ROW, width
    )
    segment = jnp.where(filled, jnp.sum(matched_int * local_ids[:, None], 0), -1).reshape(
        rows_dev, ROW
    )
    position = jnp.sum(matched_int * inside_at, 0).reshape(rows_dev, ROW)
    token_adv = jnp.sum(matched.astype(jnp.float32) * recv_adv.astype(jnp.float32)[:, None], 0)
    token_adv = token_adv.astype(jnp.bfloat16).reshape(rows_dev, ROW)
    query_full, keyval_full, out_full = (
        lax.all_gather(w_query, "dp", axis=1, tiled=True),
        lax.all_gather(w_keyval, "dp", axis=1, tiled=True),
        lax.all_gather(w_out, "dp", axis=1, tiled=True),
    )
    query_full = query_full[0]
    keyval_full = keyval_full[0]
    out_full = out_full[0]
    gain_row = norm_gain[0]
    per_block = 1
    block_count = rows_dev // per_block
    tick_count = block_count + sections - 1
    outputs = jnp.zeros_like(packed)
    result_rows = jnp.zeros((per_block, ROW, width), jnp.bfloat16)
    carried = result_rows
    for tick_index in range(tick_count):
        if tick_index > 0:
            carried = shifted(result_rows, "section", 1)
        if tick_index < block_count:
            fresh_rows = packed[tick_index * per_block : (tick_index + 1) * per_block]
        else:
            fresh_rows = jnp.zeros_like(carried)
        current_rows = jnp.where(section_me == 0, fresh_rows, carried)
        block_now = tick_index - section_me
        block_at = jnp.clip(block_now, 0, block_count - 1)
        segment_b = lax.dynamic_slice_in_dim(segment, block_at * per_block, per_block, 0)
        position_b = lax.dynamic_slice_in_dim(position, block_at * per_block, per_block, 0)
        result_rows = attend_block(
            current_rows, segment_b, position_b, gain_row, query_full, keyval_full, out_full
        )
        done_at = tick_index - (sections - 1)
        if done_at >= 0 and done_at < block_count:
            low_end = done_at * per_block
            kept = outputs[low_end : low_end + per_block]
            outputs = outputs.at[low_end : low_end + per_block].set(
                jnp.where(section_me == sections - 1, result_rows, kept)
            )
    final_all = spread(outputs, "section", sections - 1)
    share = width // sections
    hidden = lax.dynamic_slice_in_dim(final_all, section_me * share, share, 2)
    return (hidden, token_adv)


def solution(mesh):
    placed = (
        P("dp", None, None),
        P("dp"),
        P("dp", None),
        P("dp"),
        P("dp"),
        P("section", None),
        P("section", "dp", None),
        P("section", "dp", None),
        P("section", "dp", None),
    )
    return jax.shard_map(
        body,
        mesh=mesh,
        in_specs=placed,
        out_specs=(P("dp", None, "section"), P("dp", None)),
        check_vma=False,
    )
```

profile of v0, /device:TPU:0, one launch (start us, length us, event | category | flops | bytes accessed | tf_op | source)
XLA Modules:
  0.0 463.3 jit_solution(9574643511335552981)
XLA Ops:
  11.5 9.5 %all-reduce = s32[128]{0:T(128)S(1)} all-reduce(s32[128]{0:T(128)S(1)} %dynamic-update-slice.6), channel_id=2, replica_groups=mesh['section'=4,'dp'=8] {'dp'}, use_global_device_ids=true, to_apply=%add | all-reduce | flops 128 | bytes 1024
  25.4 13.0 %all-reduce.1 = (f32[8]{0:T(128)S(1)}, f32[8]{0:T(128)S(1)}) all-reduce(f32[8]{0:T(128)S(1)} %get-tuple-element.132, f32[8]{0:T(128)S(1)} %get-tuple-element.131), channel_id=1, replica_groups=mesh['section'=4,'dp'=8] {'dp'}, use_global_device_ids=true, to_apply=%region_28.29 | all-reduce | flops 16 | bytes 128 | tf_op jit(solution)/shard_map/psum | solution.py:115
  53.1 4.6 collective-permute-done.3
  57.7 4.2 collective-permute-done.4
  61.9 22.0 %collective-permute-done.5 = bf16[2,32,3584]{2,1,0:T(8,128)(2,1)S(1)} collective-permute-done((bf16[2,32,3584]{2,1,0:T(8,128)(2,1)S(1)}, bf16[2,32,3584]{2,1,0:T(8,128)(2,1)S(1)}, u32[]{:S(2)}, u32[]{:S(2)}) %collective-permute-start.5) | collective-permute-done | bytes 458784 | tf_op jit(solution)/shard_map/ppermute | solution.py:33
  89.2 6.0 %copy.76 = bf16[512,3584]{1,0:T(8,128)(2,1)} copy(bf16[512,3584]{0,1:T(8,128)(2,1)} %bitcast.400) | data formatting | bytes 7340032 | tf_op jit(solution)/shard_map/dot_general | solution.py:75
  99.2 35.8 %all-gather.7.cloned.1.call-done = bf16[1,3584,1792]{2,1,0:T(8,128)(2,1)} async-done(((bf16[1,448,1792]{2,1,0:T(8,128)(2,1)}), bf16[1,3584,1792]{2,1,0:T(8,128)(2,1)}) %all-gather.7.cloned.1.call-update) | async-done | bytes 12845072 | tf_op jit(solution)/shard_map/all_gather | solution.py:182
  135.0 18.3 %copy.77 = bf16[1792,3584]{1,0:T(8,128)(2,1)} copy(bf16[1792,3584]{0,1:T(8,128)(2,1)} %bitcast.399) | data formatting | bytes 25690112 | tf_op jit(solution)/shard_map/dot_general | solution.py:71
  153.3 6.6 %convolution_bitcast_fusion.4 = f32[1,128,14,128]{1,3,2,0:T(8,128)S(1)} fusion(bf16[14,128,3584]{2,1,0:T(8,128)(2,1)} %bitcast.387, f32[3584]{0:T(1024)S(1)} %convert_reduce_fusion, f32[128]{0:T(128)S(1)} %add_rsqrt_fusion.4, bf16[256,3584]{1,0:T(8,128)(2,1)S(1)} %broadcast_select_fusion.2, pred[]{:T(512)S(6)} %eq.202), kind=kOutput, calls=%fused_computation.64 | convolution fusion | flops 1646460928 | bytes 14696961 | tf_op jit(solution)/shard_map/dot_general | solution.py:71
  161.9 48.1 %all-gather.9.cloned.1.call-done = bf16[1,1792,3584]{2,1,0:T(8,128)(2,1)} async-done(((bf16[1,224,3584]{2,1,0:T(8,128)(2,1)}), bf16[1,1792,3584]{2,1,0:T(8,128)(2,1)}) %all-gather.9.cloned.1.call-update) | async-done | bytes 12845072 | tf_op jit(solution)/shard_map/all_gather | solution.py:184
  210.1 6.7 %fusion.52 = bf16[1,128,3584]{2,1,0:T(8,128)(2,1)S(1)} fusion(bf16[128,1792]{0,1:T(8,128)(2,1)S(1)} %bitcast.417, bf16[1,1792,3584]{2,1,0:T(8,128)(2,1)} %all-gather.9.cloned.1.call-done, bf16[256,3584]{1,0:T(8,128)(2,1)S(1)} %broadcast_select_fusion.2, pred[]{:T(512)S(6)} %eq.202), kind=kOutput, calls=%fused_computation.30 | convolution fusion | flops 1646002176 | bytes 15138817 | tf_op jit(solution)/shard_map/dot_general | solution.py:96
  221.0 19.4 %collective-permute-done.6 = bf16[1,128,3584]{2,1,0:T(8,128)(2,1)S(1)} collective-permute-done((bf16[1,128,3584]{2,1,0:T(8,128)(2,1)S(1)}, bf16[1,128,3584]{2,1,0:T(8,128)(2,1)S(1)}, u32[]{:S(2)}, u32[]{:S(2)}) %collective-permute-start.6) | collective-permute-done | bytes 917536 | tf_op jit(solution)/shard_map/ppermute | solution.py:39
  248.6 6.7 %fusion.40 = bf16[1,128,3584]{2,1,0:T(8,128)(2,1)S(1)} fusion(bf16[128,1792]{0,1:T(8,128)(2,1)S(1)} %bitcast.419, bf16[1,1792,3584]{2,1,0:T(8,128)(2,1)} %all-gather.9.cloned.1.call-done, bf16[1,128,3584]{2,1,0:T(8,128)(2,1)S(1)} %get-tuple-element.146), kind=kOutput, calls=%fused_computation.26 | convolution fusion | flops 1645543424 | bytes 15138816 | tf_op jit(solution)/shard_map/dot_general | solution.py:96
  255.3 4.7 %collective-permute-start.7 = (bf16[1,128,3584]{2,1,0:T(8,128)(2,1)S(1)}, bf16[1,128,3584]{2,1,0:T(8,128)(2,1)S(1)}, u32[]{:S(2)}, u32[]{:S(2)}) collective-permute-start(bf16[1,128,3584]{2,1,0:T(8,128)(2,1)S(1)} %fusion.40), channel_id=1, source_target_pairs={{0,8},{8,16},{16,24},{1,9},{9,17},{17,25},{2,10},{10,18},{18,26},{... | collective-permute-start | bytes 2752520 | tf_op jit(solution)/shard_map/ppermute | solution.py:39
  260.1 18.8 %collective-permute-done.7 = bf16[1,128,3584]{2,1,0:T(8,128)(2,1)S(1)} collective-permute-done((bf16[1,128,3584]{2,1,0:T(8,128)(2,1)S(1)}, bf16[1,128,3584]{2,1,0:T(8,128)(2,1)S(1)}, u32[]{:S(2)}, u32[]{:S(2)}) %collective-permute-start.7) | collective-permute-done | bytes 917536 | tf_op jit(solution)/shard_map/ppermute | solution.py:39
  286.0 6.5 %fusion.43 = bf16[1,128,3584]{2,1,0:T(8,128)(2,1)S(1)} fusion(bf16[128,1792]{0,1:T(8,128)(2,1)S(1)} %bitcast.420, bf16[1,1792,3584]{2,1,0:T(8,128)(2,1)} %all-gather.9.cloned.1.call-done, bf16[1,128,3584]{2,1,0:T(8,128)(2,1)S(1)} %collective-permute-done.7, pred[]{:T(512)S(6)} %eq.202), kind=kOutput, calls=%fused_computation.27 | convolution fusion | flops 1646002176 | bytes 15138817 | tf_op jit(solution)/shard_map/dot_general | solution.py:96
  292.5 4.4 collective-permute-start.8
  297.0 18.2 %collective-permute-done.8 = bf16[1,128,3584]{2,1,0:T(8,128)(2,1)S(1)} collective-permute-done((bf16[1,128,3584]{2,1,0:T(8,128)(2,1)S(1)}, bf16[1,128,3584]{2,1,0:T(8,128)(2,1)S(1)}, u32[]{:S(2)}, u32[]{:S(2)}) %collective-permute-start.8) | collective-permute-done | bytes 917536 | tf_op jit(solution)/shard_map/ppermute | solution.py:39
  318.8 6.6 %convolution_bitcast_fusion.1 = f32[1,128,14,128]{1,3,2,0:T(8,128)S(1)} fusion(bf16[14,128,3584]{2,1,0:T(8,128)(2,1)} %bitcast.388, f32[128]{0:T(128)S(1)} %add_rsqrt_fusion.1, f32[3584]{0:T(1024)S(1)} %convert_reduce_fusion, bf16[1,128,3584]{2,1,0:T(8,128)(2,1)S(1)} %collective-permute-done.8, pred[]{:T(512)S(6)} %eq.202), kind=kOutput, calls=%fused_computation.61 | convolution fusion | flops 1646460928 | bytes 14694913 | tf_op jit(solution)/shard_map/dot_general | solution.py:71
  327.2 6.8 %broadcast_select_fusion.6 = (bf16[1,128,3584]{2,1,0:T(8,128)(2,1)S(1)}, bf16[1,128,3584]{2,1,0:T(8,128)(2,1)S(1)}) fusion(pred[]{:T(512)S(6)} %eq.201, bf16[128,1792]{0,1:T(8,128)(2,1)S(1)} %bitcast.406, bf16[1,1792,3584]{2,1,0:T(8,128)(2,1)} %all-gather.9.cloned.1.call-done, bf16[1,128,3584]{2,1,0:T(8,128)(2,1)S(1)} %collective-permute-done.8, pred[]{:T(512)S(6)} %eq.202), kind=kOutput, calls=%fused_computation.116 | convolution fusion | flops 1646460928 | bytes 16056322 | tf_op jit(solution)/shard_map/dot_general | solution.py:96
  334.0 4.9 %collective-permute-start.9 = (bf16[1,128,3584]{2,1,0:T(8,128)(2,1)S(1)}, bf16[1,128,3584]{2,1,0:T(8,128)(2,1)S(1)}, u32[]{:S(2)}, u32[]{:S(2)}) collective-permute-start(bf16[1,128,3584]{2,1,0:T(8,128)(2,1)S(1)} %get-tuple-element.222), channel_id=1, source_target_pairs={{0,8},{8,16},{16,24},{1,9},{9,17},{17,25},{2,10},{10,18},{18,26},{... | collective-permute-start | bytes 2752520 | tf_op jit(solution)/shard_map/ppermute | solution.py:39
  339.0 17.1 %collective-permute-done.9 = bf16[1,128,3584]{2,1,0:T(8,128)(2,1)S(1)} collective-permute-done((bf16[1,128,3584]{2,1,0:T(8,128)(2,1)S(1)}, bf16[1,128,3584]{2,1,0:T(8,128)(2,1)S(1)}, u32[]{:S(2)}, u32[]{:S(2)}) %collective-permute-start.9) | collective-permute-done | bytes 917536 | tf_op jit(solution)/shard_map/ppermute | solution.py:39
  368.0 6.6 %fusion.55 = bf16[1,128,3584]{2,1,0:T(8,128)(2,1)S(1)} fusion(bf16[128,1792]{0,1:T(8,128)(2,1)S(1)} %bitcast.418, bf16[1,1792,3584]{2,1,0:T(8,128)(2,1)} %all-gather.9.cloned.1.call-done, pred[]{:T(512)S(6)} %eq.201, bf16[1,128,3584]{2,1,0:T(8,128)(2,1)S(1)} %collective-permute-done.9, pred[]{:T(512)S(6)} %eq.202), kind=kOutput, calls=%fused_computation.31 | convolution fusion | flops 1646460928 | bytes 15138818 | tf_op jit(solution)/shard_map/dot_general | solution.py:96
  376.0 78.7 %all-reduce.4.cloned.1.call-done = bf16[2,128,3584]{2,1,0:T(8,128)(2,1)} async-done(((bf16[2,128,3584]{2,1,0:T(8,128)(2,1)}), bf16[2,128,3584]{2,1,0:T(8,128)(2,1)}) %all-reduce.4.cloned.1.call-update) | async-done | bytes 1835024 | tf_op jit(solution)/shard_map/psum | solution.py:44
  (206 shorter events, 73.5 us)
Async XLA Ops:
  7.2 32.2 %copy-start = (bf16[8,32,3584]{2,1,0:T(8,128)(2,1)S(1)}, bf16[8,32,3584]{2,1,0:T(8,128)(2,1)}, u32[]{:S(2)}) copy-start(bf16[8,32,3584]{2,1,0:T(8,128)(2,1)} %param.15) | copy-start | bytes 5505028
  7.2 81.9 %all-gather.5.cloned.1.call-start = ((), (), s32[]{:S(2)}) async-start(), calls=%async_computation | async-start | bytes 4128768 | tf_op jit(solution)/shard_map/all_gather | solution.py:183
  8.0 127.1 %all-gather.7.cloned.1.call-start = ((), (), s32[]{:S(2)}) async-start(), calls=%async_computation.1 | async-start | bytes 14450688 | tf_op jit(solution)/shard_map/all_gather | solution.py:182
  8.7 201.3 %all-gather.9.cloned.1.call-start = ((), (), s32[]{:S(2)}) async-start(), calls=%async_computation.2 | async-start | bytes 14450688 | tf_op jit(solution)/shard_map/all_gather | solution.py:184
  9.5 445.3 %all-reduce.4.cloned.1.call-start = ((), (), s32[]{:S(2)}) async-start(), calls=%async_computation.3 | async-start | bytes 3670016 | tf_op jit(solution)/shard_map/psum | solution.py:44
  23.0 26.2 %collective-permute-start = (s32[2,3]{1,0:T(2,128)S(1)}, s32[2,3]{1,0:T(2,128)S(1)}, u32[]{:S(2)}, u32[]{:S(2)}) collective-permute-start(s32[2,3]{1,0:T(2,128)S(1)} %get-tuple-element.175), channel_id=1, source_target_pairs={{7,0},{0,1},{1,2},{2,3},{3,4},{4,5},{5,6},{6,7},{15,8},{8,9},{9,10... | collective-permute-start | bytes 80 | tf_op jit(solution)/shard_map/ppermute | solution.py:33
  23.0 28.3 %collective-permute-start.1 = (s32[2,3]{1,0:T(2,128)S(1)}, s32[2,3]{1,0:T(2,128)S(1)}, u32[]{:S(2)}, u32[]{:S(2)}) collective-permute-start(s32[2,3]{1,0:T(2,128)S(1)} %get-tuple-element.174), channel_id=1, source_target_pairs={{6,0},{7,1},{0,2},{1,3},{2,4},{3,5},{4,6},{5,7},{14,8},{15,9},{8,1... | collective-permute-start | bytes 80 | tf_op jit(solution)/shard_map/ppermute | solution.py:33
  23.9 27.4 %collective-permute-start.2 = (s32[2,3]{1,0:T(2,128)S(1)}, s32[2,3]{1,0:T(2,128)S(1)}, u32[]{:S(2)}, u32[]{:S(2)}) collective-permute-start(s32[2,3]{1,0:T(2,128)S(1)} %get-tuple-element.176), channel_id=1, source_target_pairs={{5,0},{6,1},{7,2},{0,3},{1,4},{2,5},{3,6},{4,7},{13,8},{14,9},{15,... | collective-permute-start | bytes 80 | tf_op jit(solution)/shard_map/ppermute | solution.py:33
  39.3 4.0 collective-permute-start.10
  39.3 6.5 %collective-permute-start.11 = (bf16[2]{0:T(256)(128)(2,1)S(1)}, bf16[2]{0:T(256)(128)(2,1)S(1)}, u32[]{:S(2)}, u32[]{:S(2)}) collective-permute-start(bf16[2]{0:T(256)(128)(2,1)S(1)} %get-tuple-element.208), channel_id=1, source_target_pairs={{6,0},{7,1},{0,2},{1,3},{2,4},{3,5},{4,6},{5,7},{14,8},{15,9},{8,1... | collective-permute-start | bytes 20 | tf_op jit(solution)/shard_map/ppermute | solution.py:33
  43.3 3.8 collective-permute-start.12
  45.8 11.9 %collective-permute-start.3 = (bf16[2,32,3584]{2,1,0:T(8,128)(2,1)S(1)}, bf16[2,32,3584]{2,1,0:T(8,128)(2,1)S(1)}, u32[]{:S(2)}, u32[]{:S(2)}) collective-permute-start(bf16[2,32,3584]{2,1,0:T(8,128)(2,1)S(1)} %get-tuple-element.151), channel_id=1, source_target_pairs={{7,0},{0,1},{1,2},{2,3},{3,4},{4,5},{5,6},{6,7},{15,8},{8,9},{9,10... | collective-permute-start | bytes 1376264 | tf_op jit(solution)/shard_map/ppermute | solution.py:33
  47.1 14.7 %collective-permute-start.4 = (bf16[2,32,3584]{2,1,0:T(8,128)(2,1)S(1)}, bf16[2,32,3584]{2,1,0:T(8,128)(2,1)S(1)}, u32[]{:S(2)}, u32[]{:S(2)}) collective-permute-start(bf16[2,32,3584]{2,1,0:T(8,128)(2,1)S(1)} %get-tuple-element.150), channel_id=1, source_target_pairs={{6,0},{7,1},{0,2},{1,3},{2,4},{3,5},{4,6},{5,7},{14,8},{15,9},{8,1... | collective-permute-start | bytes 1376264 | tf_op jit(solution)/shard_map/ppermute | solution.py:33
  49.1 34.8 %collective-permute-start.5 = (bf16[2,32,3584]{2,1,0:T(8,128)(2,1)S(1)}, bf16[2,32,3584]{2,1,0:T(8,128)(2,1)S(1)}, u32[]{:S(2)}, u32[]{:S(2)}) collective-permute-start(bf16[2,32,3584]{2,1,0:T(8,128)(2,1)S(1)} %get-tuple-element.152), channel_id=1, source_target_pairs={{5,0},{6,1},{7,2},{0,3},{1,4},{2,5},{3,6},{4,7},{13,8},{14,9},{15,... | collective-permute-start | bytes 1376264 | tf_op jit(solution)/shard_map/ppermute | solution.py:33
  99.1 54.2 %copy-start.5 = (f32[1,128,2,2,128]{1,4,3,2,0:T(8,128)}, f32[1,128,2,2,128]{1,4,3,2,0:T(8,128)S(1)}, u32[]{:S(2)}) copy-start(f32[1,128,2,2,128]{1,4,3,2,0:T(8,128)S(1)} %convolution_bitcast_fusion.9) | copy-start | bytes 786436
  210.1 32.0 %slice-start.2 = ((s8[12845056]{0:T(1024)(128)(4,1)}), s8[4194304]{0:T(1024)(128)(4,1)S(1)}, s32[]{:S(2)}) async-start(s8[12845056]{0:T(1024)(128)(4,1)} %bitcast.389), calls=%async_computation.6 | async-start | bytes 8388608
  216.7 23.7 %collective-permute-start.6 = (bf16[1,128,3584]{2,1,0:T(8,128)(2,1)S(1)}, bf16[1,128,3584]{2,1,0:T(8,128)(2,1)S(1)}, u32[]{:S(2)}, u32[]{:S(2)}) collective-permute-start(bf16[1,128,3584]{2,1,0:T(8,128)(2,1)S(1)} %fusion.52), channel_id=1, source_target_pairs={{0,8},{8,16},{16,24},{1,9},{9,17},{17,25},{2,10},{10,18},{18,26},{... | collective-permute-start | bytes 2752520 | tf_op jit(solution)/shard_map/ppermute | solution.py:39
  247.2 33.4 %slice-start.4 = ((s8[12845056]{0:T(1024)(128)(4,1)}), s8[4194304]{0:T(1024)(128)(4,1)S(1)}, s32[]{:S(2)}) async-start(s8[12845056]{0:T(1024)(128)(4,1)} %bitcast.392), calls=%async_computation.8 | async-start | bytes 8388608
  248.6 32.0 %slice-start.5 = ((s8[12845056]{0:T(1024)(128)(4,1)}), s8[4194304]{0:T(1024)(128)(4,1)S(1)}, s32[]{:S(2)}) async-start(s8[12845056]{0:T(1024)(128)(4,1)} %bitcast.392), calls=%async_computation.9 | async-start | bytes 8388608
  248.6 32.0 %slice-start.6 = ((s8[12845056]{0:T(1024)(128)(4,1)}), s8[4194304]{0:T(1024)(128)(4,1)S(1)}, s32[]{:S(2)}) async-start(s8[12845056]{0:T(1024)(128)(4,1)} %bitcast.392), calls=%async_computation.10 | async-start | bytes 8388608
  255.3 23.7 %collective-permute-start.7 = (bf16[1,128,3584]{2,1,0:T(8,128)(2,1)S(1)}, bf16[1,128,3584]{2,1,0:T(8,128)(2,1)S(1)}, u32[]{:S(2)}, u32[]{:S(2)}) collective-permute-start(bf16[1,128,3584]{2,1,0:T(8,128)(2,1)S(1)} %fusion.40), channel_id=1, source_target_pairs={{0,8},{8,16},{16,24},{1,9},{9,17},{17,25},{2,10},{10,18},{18,26},{... | collective-permute-start | bytes 2752520 | tf_op jit(solution)/shard_map/ppermute | solution.py:39
  292.5 22.7 %collective-permute-start.8 = (bf16[1,128,3584]{2,1,0:T(8,128)(2,1)S(1)}, bf16[1,128,3584]{2,1,0:T(8,128)(2,1)S(1)}, u32[]{:S(2)}, u32[]{:S(2)}) collective-permute-start(bf16[1,128,3584]{2,1,0:T(8,128)(2,1)S(1)} %fusion.43), channel_id=1, source_target_pairs={{0,8},{8,16},{16,24},{1,9},{9,17},{17,25},{2,10},{10,18},{18,26},{... | collective-permute-start | bytes 2752520 | tf_op jit(solution)/shard_map/ppermute | solution.py:39
  334.0 22.1 %collective-permute-start.9 = (bf16[1,128,3584]{2,1,0:T(8,128)(2,1)S(1)}, bf16[1,128,3584]{2,1,0:T(8,128)(2,1)S(1)}, u32[]{:S(2)}, u32[]{:S(2)}) collective-permute-start(bf16[1,128,3584]{2,1,0:T(8,128)(2,1)S(1)} %get-tuple-element.222), channel_id=1, source_target_pairs={{0,8},{8,16},{16,24},{1,9},{9,17},{17,25},{2,10},{10,18},{18,26},{... | collective-permute-start | bytes 2752520 | tf_op jit(solution)/shard_map/ppermute | solution.py:39
  374.6 82.0 %copy-start.1 = (bf16[8,32,3584]{2,1,0:T(8,128)(2,1)S(1)}, bf16[8,32,3584]{2,1,0:T(8,128)(2,1)}, u32[]{:S(2)}) copy-start(bf16[8,32,3584]{2,1,0:T(8,128)(2,1)} %param.15) | copy-start | bytes 5505028
  (20 other events, 383.8 us)
Sparse Core Ops, SparseCore 0:
  9.9 37.5 all-gather.4
  49.4 85.6 all-gather.6
  136.9 73.0 all-gather.8
  376.2 78.5 all-reduce.3
where the time goes:
time: 472 us; the launch traced here: 463 us
  waiting for transfers between devices  271 us (57%)
  matrix products  75.3 us (16%)
  local copies, waits for them, and re-layouts  41 us (9%)
  starting transfers between devices  27.5 us (6%)
  blocking collectives  22.5 us (5%)
  between operations  15.6 us (3%)
  other arithmetic  10.6 us (2%)
    psum x1, waiting for transfers between devices, spread(): return lax.psum(kept, axis)  78.7 us
    ppermute x4, waiting for transfers between devices, shifted(): return lax.ppermute(shard, axis, pairs)  73.5 us
    all_gather x1, waiting for transfers between devices, body(): lax.all_gather(w_out, 'dp', axis=1, tiled=True)  48.1 us
    all_gather x1, waiting for transfers between devices, body(): lax.all_gather(w_query, 'dp', axis=1, tiled=True)  35.8 us
    dot_general x5, matrix products, attend_block(): jnp.dot(mixed_heads, out_full, preferred_element_type=jnp.float32)  33.3 us
    ppermute x9, waiting for transfers between devices, from_behind(): return lax.ppermute(block, axis, route)  32.4 us
    dot_general x5, matrix products, attend_block(): jnp.dot(normed, query_full, preferred_element_type=jnp.float32)  24.3 us
    dot_general x1, local copies, waits for them, and re-layouts, attend_block(): jnp.dot(normed, query_full, preferred_element_type=jnp.float32)  18.3 us
  transfers between devices with their start and end apart: 17, of which 12 were waited for; matrix products, arithmetic and copies ran while one was open for 11% of the time, Pallas kernels for 0%

commit v1 on v0

--- a/solution.py
+++ b/solution.py
@@ -41,7 +41,7 @@
 
 def spread(value, axis, source):
     kept = jnp.where(lax.axis_index(axis) == source, value, 0).astype(value.dtype)
-    return lax.psum(kept, axis)
+    return jnp.sum(lax.all_gather(kept, axis), axis=0)
 
 
 def rotate(inputs, position):

time: 472 us -> 533 us (1.13)
  waiting for transfers between devices: 271 us -> 325 us
  other arithmetic: 10.6 us -> 16.9 us
    all_gather x0 -> x1, waiting for transfers between devices: none -> 134 us  [spread(): return jnp.sum(lax.all_gather(kept, axis), axis=0)]
    psum x1 -> x0, waiting for transfers between devices: 78.7 us -> none  [spread(): return lax.psum(kept, axis)]
    reduce_sum x0 -> x1, other arithmetic: none -> 6.18 us  [spread(): return jnp.sum(lax.all_gather(kept, axis), axis=0)]
  transfers between devices with their start and end apart: 17 -> 17, of which waited for: 12 -> 12; matrix products, arithmetic and copies ran while one was open for 11% -> 10% of each run, Pallas kernels for 0% -> 0%
where the time goes in v1:
time: 533 us; the launch traced here: 524 us
  waiting for transfers between devices  325 us (61%)
  matrix products  75.2 us (14%)
  local copies, waits for them, and re-layouts  41 us (8%)
  starting transfers between devices  27.5 us (5%)
  blocking collectives  22.5 us (4%)
  other arithmetic  16.9 us (3%)
  between operations  15.6 us (3%)
    all_gather x1, waiting for transfers between devices, spread(): return jnp.sum(lax.all_gather(kept, axis), axis=0)  134 us
    ppermute x4, waiting for transfers between devices, shifted(): return lax.ppermute(shard, axis, pairs)  73.4 us
    all_gather x1, waiting for transfers between devices, body(): lax.all_gather(w_out, 'dp', axis=1, tiled=True)  48.1 us
    all_gather x1, waiting for transfers between devices, body(): lax.all_gather(w_query, 'dp', axis=1, tiled=True)  35.8 us
    dot_general x5, matrix products, attend_block(): jnp.dot(mixed_heads, out_full, preferred_element_type=jnp.float32)  33.2 us
    ppermute x9, waiting for transfers between devices, from_behind(): return lax.ppermute(block, axis, route)  32.4 us
    dot_general x5, matrix products, attend_block(): jnp.dot(normed, query_full, preferred_element_type=jnp.float32)  24.2 us
    dot_general x1, local copies, waits for them, and re-layouts, attend_block(): jnp.dot(normed, query_full, preferred_element_type=jnp.float32)  18.3 us
  transfers between devices with their start and end apart: 17, of which 12 were waited for; matrix products, arithmetic and copies ran while one was open for 10% of the time, Pallas kernels for 0%

profile of v1, /device:TPU:0, one launch (start us, length us, event | category | flops | bytes accessed | tf_op | source)
XLA Modules:
  0.0 524.3 jit_solution(14198956995876813481)
XLA Ops:
  11.5 9.5 %all-reduce = s32[128]{0:T(128)S(1)} all-reduce(s32[128]{0:T(128)S(1)} %dynamic-update-slice.6), channel_id=2, replica_groups=mesh['section'=4,'dp'=8] {'dp'}, use_global_device_ids=true, to_apply=%add | all-reduce | flops 128 | bytes 1024
  25.4 13.0 %all-reduce.1 = (f32[8]{0:T(128)S(1)}, f32[8]{0:T(128)S(1)}) all-reduce(f32[8]{0:T(128)S(1)} %get-tuple-element.132, f32[8]{0:T(128)S(1)} %get-tuple-element.131), channel_id=1, replica_groups=mesh['section'=4,'dp'=8] {'dp'}, use_global_device_ids=true, to_apply=%region_28.29 | all-reduce | flops 16 | bytes 128 | tf_op jit(solution)/shard_map/psum | solution.py:115
  53.1 4.6 collective-permute-done.3
  61.9 22.0 %collective-permute-done.5 = bf16[2,32,3584]{2,1,0:T(8,128)(2,1)S(1)} collective-permute-done((bf16[2,32,3584]{2,1,0:T(8,128)(2,1)S(1)}, bf16[2,32,3584]{2,1,0:T(8,128)(2,1)S(1)}, u32[]{:S(2)}, u32[]{:S(2)}) %collective-permute-start.5) | collective-permute-done | bytes 458784 | tf_op jit(solution)/shard_map/ppermute | solution.py:33
  89.2 6.0 %copy.105 = bf16[512,3584]{1,0:T(8,128)(2,1)} copy(bf16[512,3584]{0,1:T(8,128)(2,1)} %bitcast.406) | data formatting | bytes 7340032 | tf_op jit(solution)/shard_map/dot_general | solution.py:75
  99.2 35.8 %all-gather.8.cloned.1.call-done = bf16[1,3584,1792]{2,1,0:T(8,128)(2,1)} async-done(((bf16[1,448,1792]{2,1,0:T(8,128)(2,1)}), bf16[1,3584,1792]{2,1,0:T(8,128)(2,1)}) %all-gather.8.cloned.1.call-update) | async-done | bytes 12845072 | tf_op jit(solution)/shard_map/all_gather | solution.py:182
  135.0 18.3 %copy.106 = bf16[1792,3584]{1,0:T(8,128)(2,1)} copy(bf16[1792,3584]{0,1:T(8,128)(2,1)} %bitcast.405) | data formatting | bytes 25690112 | tf_op jit(solution)/shard_map/dot_general | solution.py:71
  153.3 6.6 %convolution_bitcast_fusion.4 = f32[1,128,14,128]{1,3,2,0:T(8,128)S(1)} fusion(bf16[14,128,3584]{2,1,0:T(8,128)(2,1)} %bitcast.393, f32[3584]{0:T(1024)S(1)} %convert_reduce_fusion, f32[128]{0:T(128)S(1)} %add_rsqrt_fusion.4, bf16[256,3584]{1,0:T(8,128)(2,1)S(1)} %broadcast_select_fusion.2, pred[]{:T(512)S(6)} %eq.202), kind=kOutput, calls=%fused_computation.65 | convolution fusion | flops 1646460928 | bytes 14696961 | tf_op jit(solution)/shard_map/dot_general | solution.py:71
  161.9 48.1 %all-gather.10.cloned.1.call-done = bf16[1,1792,3584]{2,1,0:T(8,128)(2,1)} async-done(((bf16[1,224,3584]{2,1,0:T(8,128)(2,1)}), bf16[1,1792,3584]{2,1,0:T(8,128)(2,1)}) %all-gather.10.cloned.1.call-update) | async-done | bytes 12845072 | tf_op jit(solution)/shard_map/all_gather | solution.py:184
  210.1 6.7 %fusion.52 = bf16[1,128,3584]{2,1,0:T(8,128)(2,1)S(1)} fusion(bf16[128,1792]{0,1:T(8,128)(2,1)S(1)} %bitcast.422, bf16[1,1792,3584]{2,1,0:T(8,128)(2,1)} %all-gather.10.cloned.1.call-done, bf16[256,3584]{1,0:T(8,128)(2,1)S(1)} %broadcast_select_fusion.2, pred[]{:T(512)S(6)} %eq.202), kind=kOutput, calls=%fused_computation.30 | convolution fusion | flops 1646002176 | bytes 15138817 | tf_op jit(solution)/shard_map/dot_general | solution.py:96
  221.0 19.4 %collective-permute-done.6 = bf16[1,128,3584]{2,1,0:T(8,128)(2,1)S(1)} collective-permute-done((bf16[1,128,3584]{2,1,0:T(8,128)(2,1)S(1)}, bf16[1,128,3584]{2,1,0:T(8,128)(2,1)S(1)}, u32[]{:S(2)}, u32[]{:S(2)}) %collective-permute-start.6) | collective-permute-done | bytes 917536 | tf_op jit(solution)/shard_map/ppermute | solution.py:39
  248.6 6.7 %fusion.40 = bf16[1,128,3584]{2,1,0:T(8,128)(2,1)S(1)} fusion(bf16[128,1792]{0,1:T(8,128)(2,1)S(1)} %bitcast.424, bf16[1,1792,3584]{2,1,0:T(8,128)(2,1)} %all-gather.10.cloned.1.call-done, bf16[1,128,3584]{2,1,0:T(8,128)(2,1)S(1)} %get-tuple-element.146), kind=kOutput, calls=%fused_computation.26 | convolution fusion | flops 1645543424 | bytes 15138816 | tf_op jit(solution)/shard_map/dot_general | solution.py:96
  255.3 4.7 collective-permute-start.7
  260.1 18.8 %collective-permute-done.7 = bf16[1,128,3584]{2,1,0:T(8,128)(2,1)S(1)} collective-permute-done((bf16[1,128,3584]{2,1,0:T(8,128)(2,1)S(1)}, bf16[1,128,3584]{2,1,0:T(8,128)(2,1)S(1)}, u32[]{:S(2)}, u32[]{:S(2)}) %collective-permute-start.7) | collective-permute-done | bytes 917536 | tf_op jit(solution)/shard_map/ppermute | solution.py:39
  286.0 6.5 %fusion.43 = bf16[1,128,3584]{2,1,0:T(8,128)(2,1)S(1)} fusion(bf16[128,1792]{0,1:T(8,128)(2,1)S(1)} %bitcast.425, bf16[1,1792,3584]{2,1,0:T(8,128)(2,1)} %all-gather.10.cloned.1.call-done, bf16[1,128,3584]{2,1,0:T(8,128)(2,1)S(1)} %collective-permute-done.7, pred[]{:T(512)S(6)} %eq.202), kind=kOutput, calls=%fused_computation.27 | convolution fusion | flops 1646002176 | bytes 15138817 | tf_op jit(solution)/shard_map/dot_general | solution.py:96
  292.5 4.4 collective-permute-start.8
  297.1 18.1 %collective-permute-done.8 = bf16[1,128,3584]{2,1,0:T(8,128)(2,1)S(1)} collective-permute-done((bf16[1,128,3584]{2,1,0:T(8,128)(2,1)S(1)}, bf16[1,128,3584]{2,1,0:T(8,128)(2,1)S(1)}, u32[]{:S(2)}, u32[]{:S(2)}) %collective-permute-start.8) | collective-permute-done | bytes 917536 | tf_op jit(solution)/shard_map/ppermute | solution.py:39
  318.8 6.6 %convolution_bitcast_fusion.1 = f32[1,128,14,128]{1,3,2,0:T(8,128)S(1)} fusion(bf16[14,128,3584]{2,1,0:T(8,128)(2,1)} %bitcast.394, f32[128]{0:T(128)S(1)} %add_rsqrt_fusion.1, f32[3584]{0:T(1024)S(1)} %convert_reduce_fusion, bf16[1,128,3584]{2,1,0:T(8,128)(2,1)S(1)} %collective-permute-done.8, pred[]{:T(512)S(6)} %eq.202), kind=kOutput, calls=%fused_computation.62 | convolution fusion | flops 1646460928 | bytes 14694913 | tf_op jit(solution)/shard_map/dot_general | solution.py:71
  327.2 6.7 %fusion.46 = bf16[1,128,3584]{2,1,0:T(8,128)(2,1)S(1)} fusion(bf16[128,1792]{0,1:T(8,128)(2,1)S(1)} %bitcast.426, bf16[1,1792,3584]{2,1,0:T(8,128)(2,1)} %all-gather.10.cloned.1.call-done, bf16[1,128,3584]{2,1,0:T(8,128)(2,1)S(1)} %collective-permute-done.8, pred[]{:T(512)S(6)} %eq.202), kind=kOutput, calls=%fused_computation.28 | convolution fusion | flops 1646002176 | bytes 15138817 | tf_op jit(solution)/shard_map/dot_general | solution.py:96
  333.9 4.9 collective-permute-start.9
  338.9 17.1 %collective-permute-done.9 = bf16[1,128,3584]{2,1,0:T(8,128)(2,1)S(1)} collective-permute-done((bf16[1,128,3584]{2,1,0:T(8,128)(2,1)S(1)}, bf16[1,128,3584]{2,1,0:T(8,128)(2,1)S(1)}, u32[]{:S(2)}, u32[]{:S(2)}) %collective-permute-start.9) | collective-permute-done | bytes 917536 | tf_op jit(solution)/shard_map/ppermute | solution.py:39
  367.9 6.6 %fusion.58 = bf16[1,1,128,3584]{3,2,1,0:T(8,128)(2,1)S(1)} fusion(bf16[128,1792]{0,1:T(8,128)(2,1)S(1)} %bitcast.423, bf16[1,1792,3584]{2,1,0:T(8,128)(2,1)} %all-gather.10.cloned.1.call-done, pred[]{:T(512)S(6)} %eq.201, bf16[1,128,3584]{2,1,0:T(8,128)(2,1)S(1)} %collective-permute-done.9, pred[]{:T(512)S(6)} %eq.202), kind=kOutput, calls=%fused_computation.32 | convolution fusion | flops 1646460928 | bytes 15138818 | tf_op jit(solution)/shard_map/dot_general | solution.py:96
  376.0 133.5 %all-gather.12.cloned.1.call-done = bf16[4,2,128,3584]{3,2,1,0:T(8,128)(2,1)} async-done(((bf16[1,2,128,3584]{3,2,1,0:T(8,128)(2,1)}), bf16[4,2,128,3584]{3,2,1,0:T(8,128)(2,1)}) %all-gather.12.cloned.1.call-update) | async-done | bytes 7340048 | tf_op jit(solution)/shard_map/all_gather | solution.py:44
  509.6 6.2 %reduce_sum.244 = bf16[2,128,3584]{2,1,0:T(8,128)(2,1)} reduce(bf16[4,2,128,3584]{3,2,1,0:T(8,128)(2,1)} %all-gather.12.cloned.1.call-done, bf16[]{:T(256)} %constant.180.clone.1), dimensions={0}, to_apply=%region_26.27 | reduce | flops 2752512 | bytes 9175042 | tf_op jit(solution)/shard_map/reduce_sum | solution.py:44
  (208 shorter events, 77.8 us)
Async XLA Ops:
  7.2 32.2 %copy-start = (bf16[8,32,3584]{2,1,0:T(8,128)(2,1)S(1)}, bf16[8,32,3584]{2,1,0:T(8,128)(2,1)}, u32[]{:S(2)}) copy-start(bf16[8,32,3584]{2,1,0:T(8,128)(2,1)} %param.15) | copy-start | bytes 5505028
  7.2 81.9 %all-gather.6.cloned.1.call-start = ((), (), s32[]{:S(2)}) async-start(), calls=%async_computation | async-start | bytes 4128768 | tf_op jit(solution)/shard_map/all_gather | solution.py:183
  8.0 127.1 %all-gather.8.cloned.1.call-start = ((), (), s32[]{:S(2)}) async-start(), calls=%async_computation.1 | async-start | bytes 14450688 | tf_op jit(solution)/shard_map/all_gather | solution.py:182
  8.7 201.3 %all-gather.10.cloned.1.call-start = ((), (), s32[]{:S(2)}) async-start(), calls=%async_computation.2 | async-start | bytes 14450688 | tf_op jit(solution)/shard_map/all_gather | solution.py:184
  9.5 500.1 %all-gather.12.cloned.1.call-start = ((), (), s32[]{:S(2)}) async-start(), calls=%async_computation.3 | async-start | bytes 9175040 | tf_op jit(solution)/shard_map/all_gather | solution.py:44
  23.0 26.2 %collective-permute-start = (s32[2,3]{1,0:T(2,128)S(1)}, s32[2,3]{1,0:T(2,128)S(1)}, u32[]{:S(2)}, u32[]{:S(2)}) collective-permute-start(s32[2,3]{1,0:T(2,128)S(1)} %get-tuple-element.175), channel_id=1, source_target_pairs={{7,0},{0,1},{1,2},{2,3},{3,4},{4,5},{5,6},{6,7},{15,8},{8,9},{9,10... | collective-permute-start | bytes 80 | tf_op jit(solution)/shard_map/ppermute | solution.py:33
  23.0 28.3 %collective-permute-start.1 = (s32[2,3]{1,0:T(2,128)S(1)}, s32[2,3]{1,0:T(2,128)S(1)}, u32[]{:S(2)}, u32[]{:S(2)}) collective-permute-start(s32[2,3]{1,0:T(2,128)S(1)} %get-tuple-element.174), channel_id=1, source_target_pairs={{6,0},{7,1},{0,2},{1,3},{2,4},{3,5},{4,6},{5,7},{14,8},{15,9},{8,1... | collective-permute-start | bytes 80 | tf_op jit(solution)/shard_map/ppermute | solution.py:33
  23.9 27.4 %collective-permute-start.2 = (s32[2,3]{1,0:T(2,128)S(1)}, s32[2,3]{1,0:T(2,128)S(1)}, u32[]{:S(2)}, u32[]{:S(2)}) collective-permute-start(s32[2,3]{1,0:T(2,128)S(1)} %get-tuple-element.176), channel_id=1, source_target_pairs={{5,0},{6,1},{7,2},{0,3},{1,4},{2,5},{3,6},{4,7},{13,8},{14,9},{15,... | collective-permute-start | bytes 80 | tf_op jit(solution)/shard_map/ppermute | solution.py:33
  39.3 4.0 collective-permute-start.10
  39.3 6.5 %collective-permute-start.11 = (bf16[2]{0:T(256)(128)(2,1)S(1)}, bf16[2]{0:T(256)(128)(2,1)S(1)}, u32[]{:S(2)}, u32[]{:S(2)}) collective-permute-start(bf16[2]{0:T(256)(128)(2,1)S(1)} %get-tuple-element.208), channel_id=1, source_target_pairs={{6,0},{7,1},{0,2},{1,3},{2,4},{3,5},{4,6},{5,7},{14,8},{15,9},{8,1... | collective-permute-start | bytes 20 | tf_op jit(solution)/shard_map/ppermute | solution.py:33
  43.3 3.8 collective-permute-start.12
  45.8 11.9 %collective-permute-start.3 = (bf16[2,32,3584]{2,1,0:T(8,128)(2,1)S(1)}, bf16[2,32,3584]{2,1,0:T(8,128)(2,1)S(1)}, u32[]{:S(2)}, u32[]{:S(2)}) collective-permute-start(bf16[2,32,3584]{2,1,0:T(8,128)(2,1)S(1)} %get-tuple-element.151), channel_id=1, source_target_pairs={{7,0},{0,1},{1,2},{2,3},{3,4},{4,5},{5,6},{6,7},{15,8},{8,9},{9,10... | collective-permute-start | bytes 1376264 | tf_op jit(solution)/shard_map/ppermute | solution.py:33
  47.1 14.7 %collective-permute-start.4 = (bf16[2,32,3584]{2,1,0:T(8,128)(2,1)S(1)}, bf16[2,32,3584]{2,1,0:T(8,128)(2,1)S(1)}, u32[]{:S(2)}, u32[]{:S(2)}) collective-permute-start(bf16[2,32,3584]{2,1,0:T(8,128)(2,1)S(1)} %get-tuple-element.150), channel_id=1, source_target_pairs={{6,0},{7,1},{0,2},{1,3},{2,4},{3,5},{4,6},{5,7},{14,8},{15,9},{8,1... | collective-permute-start | bytes 1376264 | tf_op jit(solution)/shard_map/ppermute | solution.py:33
  49.1 34.8 %collective-permute-start.5 = (bf16[2,32,3584]{2,1,0:T(8,128)(2,1)S(1)}, bf16[2,32,3584]{2,1,0:T(8,128)(2,1)S(1)}, u32[]{:S(2)}, u32[]{:S(2)}) collective-permute-start(bf16[2,32,3584]{2,1,0:T(8,128)(2,1)S(1)} %get-tuple-element.152), channel_id=1, source_target_pairs={{5,0},{6,1},{7,2},{0,3},{1,4},{2,5},{3,6},{4,7},{13,8},{14,9},{15,... | collective-permute-start | bytes 1376264 | tf_op jit(solution)/shard_map/ppermute | solution.py:33
  99.1 54.2 %copy-start.5 = (f32[1,128,2,2,128]{1,4,3,2,0:T(8,128)}, f32[1,128,2,2,128]{1,4,3,2,0:T(8,128)S(1)}, u32[]{:S(2)}) copy-start(f32[1,128,2,2,128]{1,4,3,2,0:T(8,128)S(1)} %convolution_bitcast_fusion.9) | copy-start | bytes 786436
  210.1 32.0 %slice-start.2 = ((s8[12845056]{0:T(1024)(128)(4,1)}), s8[4194304]{0:T(1024)(128)(4,1)S(1)}, s32[]{:S(2)}) async-start(s8[12845056]{0:T(1024)(128)(4,1)} %bitcast.395), calls=%async_computation.6 | async-start | bytes 8388608
  216.7 23.7 %collective-permute-start.6 = (bf16[1,128,3584]{2,1,0:T(8,128)(2,1)S(1)}, bf16[1,128,3584]{2,1,0:T(8,128)(2,1)S(1)}, u32[]{:S(2)}, u32[]{:S(2)}) collective-permute-start(bf16[1,128,3584]{2,1,0:T(8,128)(2,1)S(1)} %fusion.52), channel_id=1, source_target_pairs={{0,8},{8,16},{16,24},{1,9},{9,17},{17,25},{2,10},{10,18},{18,26},{... | collective-permute-start | bytes 2752520 | tf_op jit(solution)/shard_map/ppermute | solution.py:39
  247.2 33.4 %slice-start.4 = ((s8[12845056]{0:T(1024)(128)(4,1)}), s8[4194304]{0:T(1024)(128)(4,1)S(1)}, s32[]{:S(2)}) async-start(s8[12845056]{0:T(1024)(128)(4,1)} %bitcast.398), calls=%async_computation.8 | async-start | bytes 8388608
  248.6 32.0 %slice-start.5 = ((s8[12845056]{0:T(1024)(128)(4,1)}), s8[4194304]{0:T(1024)(128)(4,1)S(1)}, s32[]{:S(2)}) async-start(s8[12845056]{0:T(1024)(128)(4,1)} %bitcast.398), calls=%async_computation.9 | async-start | bytes 8388608
  248.6 32.0 %slice-start.6 = ((s8[12845056]{0:T(1024)(128)(4,1)}), s8[4194304]{0:T(1024)(128)(4,1)S(1)}, s32[]{:S(2)}) async-start(s8[12845056]{0:T(1024)(128)(4,1)} %bitcast.398), calls=%async_computation.10 | async-start | bytes 8388608
  248.6 32.0 %slice-start.7 = ((s8[12845056]{0:T(1024)(128)(4,1)}), s8[262144]{0:T(1024)(128)(4,1)S(1)}, s32[]{:S(2)}) async-start(s8[12845056]{0:T(1024)(128)(4,1)} %bitcast.398), calls=%async_computation.11 | async-start | bytes 524288
  255.3 23.7 %collective-permute-start.7 = (bf16[1,128,3584]{2,1,0:T(8,128)(2,1)S(1)}, bf16[1,128,3584]{2,1,0:T(8,128)(2,1)S(1)}, u32[]{:S(2)}, u32[]{:S(2)}) collective-permute-start(bf16[1,128,3584]{2,1,0:T(8,128)(2,1)S(1)} %fusion.40), channel_id=1, source_target_pairs={{0,8},{8,16},{16,24},{1,9},{9,17},{17,25},{2,10},{10,18},{18,26},{... | collective-permute-start | bytes 2752520 | tf_op jit(solution)/shard_map/ppermute | solution.py:39
  292.5 22.7 %collective-permute-start.8 = (bf16[1,128,3584]{2,1,0:T(8,128)(2,1)S(1)}, bf16[1,128,3584]{2,1,0:T(8,128)(2,1)S(1)}, u32[]{:S(2)}, u32[]{:S(2)}) collective-permute-start(bf16[1,128,3584]{2,1,0:T(8,128)(2,1)S(1)} %fusion.43), channel_id=1, source_target_pairs={{0,8},{8,16},{16,24},{1,9},{9,17},{17,25},{2,10},{10,18},{18,26},{... | collective-permute-start | bytes 2752520 | tf_op jit(solution)/shard_map/ppermute | solution.py:39
  333.9 22.1 %collective-permute-start.9 = (bf16[1,128,3584]{2,1,0:T(8,128)(2,1)S(1)}, bf16[1,128,3584]{2,1,0:T(8,128)(2,1)S(1)}, u32[]{:S(2)}, u32[]{:S(2)}) collective-permute-start(bf16[1,128,3584]{2,1,0:T(8,128)(2,1)S(1)} %fusion.46), channel_id=1, source_target_pairs={{0,8},{8,16},{16,24},{1,9},{9,17},{17,25},{2,10},{10,18},{18,26},{... | collective-permute-start | bytes 2752520 | tf_op jit(solution)/shard_map/ppermute | solution.py:39
  (20 other events, 352.7 us)
Sparse Core Ops, SparseCore 0:
  9.9 37.5 all-gather.5
  49.4 85.6 all-gather.7
  136.9 73.0 all-gather.9
  376.1 133.3 all-gather.11
